TPU v7x, 32 devices: a whole 2x2x4 slice. The times are simulated.
32 devices in a mesh: head: 4 (over x, core), seq: 8 (over z, y).
Axes of the slice: x: 2, y: 2, z: 4, core: 2. Of those that a mesh axis runs over, the one named last changes fastest.
Arguments:
- queries: bfloat16 [2048, 4096], P('seq', 'head'), may hold values from -160 to 160
- encodings: bfloat16 [24, 128, 1024], P('seq', None, 'head'), may hold values from -6 to 6
- kv_weight: bfloat16 [2, 1024, 4096], P(None, None, 'head'), may hold values from -0.1875 to 0.1875
- grad_out: bfloat16 [2048, 4096], P('seq', 'head'), may hold values from -6 to 6
- neighbour_owner: int32 [32, 2], replicated, may hold values from 0 to 7, all different within a row; in each aligned block of 4 rows (0 to 3, 4 to 7, ...) at most 2 rows name the same one
- neighbour_slot: int32 [32, 2], replicated, may hold values from 0 to 2
Outputs:
- attended: bfloat16 [2048, 4096], P('seq', 'head')
- query_grad: bfloat16 [32, 64, 4096], P('seq', 'head')
- encoding_grad: bfloat16 [24, 128, 1024], P('seq', None, 'head')
Inputs may be any that keep to these rules, and one draw needn't show every extreme that they name: `neighbour_owner`: the 2 owners of one span differ. Among the 4 spans of one index of seq (aligned blocks of rows), no owner is named more than 2 times, and in every draw some owner is named exactly 2 times.
All inputs are finite; a program needn't handle non-finite values.
Results may differ from a plain program's by a relative error of at most 0.019.
The roundings to bfloat16 on the way count: a program that leaves them out, or rounds other values in their place, can miss the bound.
Values may be sent and summed in bfloat16 or wider, within the bound.
A program may use at most 64 MiB of HBM per device.

v0:
```python
import jax
import jax.numpy as jnp
from jax import lax
from jax.sharding import PartitionSpec as P

HEAD_DIM = 128
SPAN = 64
NEIGHBOURS = 2
NEIGHBOUR_LEN = 128


def passed_along(array, axis, by):
    count = lax.axis_size(axis)
    pairs = [(i, i + by) for i in range(count) if 0 <= i + by < count]
    return lax.ppermute(array, axis, pairs)


def per_device(queries, encodings, kv_weight, grad_out, neighbour_owner, neighbour_slot):
    seq_count = lax.axis_size("seq")
    seq_index = lax.axis_index("seq")
    scale = HEAD_DIM ** (-0.5)
    token_rows = queries.shape[0]
    local_width = queries.shape[1]
    local_heads = local_width // HEAD_DIM
    spans_local = token_rows // SPAN
    groups = spans_local + 1
    requests = spans_local * NEIGHBOURS
    capacity = max(2, (requests + seq_count - 1) // seq_count)
    tile_rows = encodings.shape[0]
    slice_width = encodings.shape[2]
    window = NEIGHBOURS * NEIGHBOUR_LEN
    owners_all = neighbour_owner.reshape(seq_count, requests)
    slots_all = neighbour_slot.reshape(seq_count, requests)
    order = jnp.arange(requests)
    earlier = order[:, None] > order[None, :]
    same_owner = owners_all[:, :, None] == owners_all[:, None, :]
    ranks_all = jnp.sum((same_owner & earlier[None]).astype(jnp.int32), axis=2)
    my_owner = lax.dynamic_index_in_dim(owners_all, seq_index, 0, keepdims=False)
    my_rank = lax.dynamic_index_in_dim(ranks_all, seq_index, 0, keepdims=False)
    slot_place = my_owner * capacity + my_rank
    matched = (owners_all == seq_index)[:, :, None] & (
        ranks_all[:, :, None] == jnp.arange(capacity)[None, None, :]
    )
    matched = matched.astype(jnp.int32)
    chosen = jnp.sum(matched * slots_all[:, :, None], axis=1).reshape(-1)
    filled = jnp.sum(matched, axis=1).reshape(-1)
    target = jnp.where(filled > 0, chosen, tile_rows)
    outgoing = jnp.where(filled[:, None, None] > 0, encodings[chosen], jnp.zeros((), jnp.bfloat16))
    outgoing = outgoing.reshape(seq_count, capacity, NEIGHBOUR_LEN, slice_width)
    incoming = lax.all_to_all(outgoing, "seq", split_axis=0, concat_axis=0, tiled=True)
    picked = incoming.reshape(seq_count * capacity, NEIGHBOUR_LEN, slice_width)[slot_place]
    features = lax.all_gather(picked, "head", axis=2, tiled=True)
    projected = jnp.einsum(
        "rle,ced->crld", features, kv_weight, preferred_element_type=jnp.float32
    ).astype(jnp.bfloat16)
    by_span = projected.reshape(2, spans_local, window, local_width)
    carried = passed_along(by_span[:, -1], "seq", 1)
    extended = jnp.concatenate([carried[:, None], by_span], axis=1)
    extended = extended.reshape(2, groups, window, local_heads, HEAD_DIM)
    key_block = extended[0]
    value_block = extended[1]

    def padded_groups(rows):
        padded = jnp.concatenate(
            [
                jnp.zeros((1, local_width), rows.dtype),
                rows,
                jnp.zeros((SPAN - 1, local_width), rows.dtype),
            ],
            0,
        )
        return padded.reshape(groups, SPAN, local_heads, HEAD_DIM)

    query_pad = padded_groups(queries)
    grad_pad = padded_groups(grad_out)
    scores = (
        jnp.einsum("gqhd,gkhd->ghqk", query_pad, key_block, preferred_element_type=jnp.float32)
        * scale
    )
    top = jnp.max(scores, axis=-1, keepdims=True)
    expo = jnp.exp(scores - top)
    probs = expo / jnp.sum(expo, axis=-1, keepdims=True)
    probs_half = probs.astype(jnp.bfloat16)
    output = jnp.einsum(
        "ghqk,gkhd->gqhd", probs_half, value_block, preferred_element_type=jnp.float32
    )
    attended = output.reshape(groups * SPAN, local_width)[1 : 1 + token_rows].astype(jnp.bfloat16)
    dprob = jnp.einsum("gqhd,gkhd->ghqk", grad_pad, value_block, preferred_element_type=jnp.float32)
    delta = jnp.sum(probs * dprob, axis=-1, keepdims=True)
    dscore = (probs * (dprob - delta)).astype(jnp.bfloat16)
    qgrad = (
        jnp.einsum("ghqk,gkhd->gqhd", dscore, key_block, preferred_element_type=jnp.float32) * scale
    )
    kgrad = (
        jnp.einsum("ghqk,gqhd->gkhd", dscore, query_pad, preferred_element_type=jnp.float32) * scale
    )
    vgrad = jnp.einsum("ghqk,gqhd->gkhd", probs_half, grad_pad, preferred_element_type=jnp.float32)
    qgrad_rows = qgrad.reshape(groups * SPAN, local_width)[1 : 1 + token_rows].astype(jnp.bfloat16)
    qgrad_rows = qgrad_rows.reshape(spans_local, SPAN, local_width)
    query_grad = lax.all_to_all(qgrad_rows, "head", split_axis=1, concat_axis=2, tiled=True)
    kv_grad = jnp.stack([kgrad, vgrad], 0).reshape(2, groups, window, local_width)
    returned = passed_along(kv_grad[:, 0], "seq", -1)
    own_grad = kv_grad[:, 1:].at[:, -1].add(returned)
    grad_half = own_grad.astype(jnp.bfloat16).reshape(2, requests, NEIGHBOUR_LEN, local_width)
    flat_half = grad_half.reshape(2, requests * NEIGHBOUR_LEN, local_width)
    term = jnp.einsum("cnd,ced->ne", flat_half, kv_weight, preferred_element_type=jnp.float32)
    term = term.reshape(requests, NEIGHBOUR_LEN, -1)
    request_grad = lax.psum_scatter(term, "head", scatter_dimension=2, tiled=True)
    outgoing_grad = jnp.zeros((seq_count * capacity, NEIGHBOUR_LEN, slice_width), jnp.float32)
    outgoing_grad = outgoing_grad.at[slot_place].set(request_grad)
    outgoing_grad = outgoing_grad.reshape(seq_count, capacity, NEIGHBOUR_LEN, slice_width)
    incoming_grad = lax.all_to_all(outgoing_grad, "seq", split_axis=0, concat_axis=0, tiled=True)
    summed = jnp.zeros((tile_rows + 1, NEIGHBOUR_LEN, slice_width), jnp.float32)
    summed = summed.at[target].add(
        incoming_grad.reshape(seq_count * capacity, NEIGHBOUR_LEN, slice_width)
    )
    tile_grad = summed[:tile_rows]
    return (attended, query_grad, tile_grad.astype(jnp.bfloat16))


def solution(mesh):
    in_specs = (
        P("seq", "head"),
        P("seq", None, "head"),
        P(None, None, "head"),
        P("seq", "head"),
        P(),
        P(),
    )
    out_specs = (P("seq", "head"), P("seq", "head", None), P("seq", None, "head"))
    return jax.shard_map(
        per_device, mesh=mesh, in_specs=in_specs, out_specs=out_specs, check_vma=False
    )
```

profile of v0, /device:TPU:0, one launch (start us, length us, event | category | flops | bytes accessed | tf_op | source)
XLA Modules:
  0.0 320.8 jit_solution(1670462678393541136)
XLA Ops:
  7.2 0.8 copy.79
  8.0 0.1 reshape.216
  8.1 0.3 convert_reduce_fusion
  8.4 0.8 copy.81
  9.1 0.1 mul.51
  9.2 0.2 convert_reduce_fusion.1
  9.4 0.1 copy.80
  9.5 0.1 gt.40
  9.6 0.1 copy.82
  9.6 0.1 reshape.217
  9.8 0.6 gather_fusion
  10.4 1.1 broadcast_select_fusion
  11.5 7.3 %all-to-all-start = ((bf16[8,2,128,256]{3,2,1,0:T(8,128)(2,1)}), bf16[8,2,128,256]{3,2,1,0:T(8,128)(2,1)S(1)}, u32[]{:S(2)}, u32[]{:S(2)}) async-start(bf16[8,2,128,256]{3,2,1,0:T(8,128)(2,1)} %broadcast_select_fusion), calls=%async_computation | async-start | bytes 2097152 | tf_op jit(solution)/shard_map/all_to_all | solution.py:50
  18.9 25.7 %all-to-all-done = bf16[8,2,128,256]{3,2,1,0:T(8,128)(2,1)S(1)} async-done(((bf16[8,2,128,256]{3,2,1,0:T(8,128)(2,1)}), bf16[8,2,128,256]{3,2,1,0:T(8,128)(2,1)S(1)}, u32[]{:S(2)}, u32[]{:S(2)}) %all-to-all-start) | async-done | bytes 1048608 | tf_op jit(solution)/shard_map/all_to_all | solution.py:50
  44.5 1.4 gather_fusion.1
  46.0 22.0 %all-gather.3.cloned.1.call-done = bf16[8,128,1024]{2,1,0:T(8,128)(2,1)} async-done(((bf16[8,128,256]{2,1,0:T(8,128)(2,1)}), bf16[8,128,1024]{2,1,0:T(8,128)(2,1)}) %all-gather.3.cloned.1.call-update) | async-done | bytes 2097168 | tf_op jit(solution)/shard_map/all_gather | solution.py:52
  67.9 7.3 %convert_bitcast_fusion = bf16[2,8,128,1024]{3,2,0,1:T(8,128)(2,1)S(1)} fusion(bf16[2,1024,1024]{2,1,0:T(8,128)(2,1)} %param.10, bf16[8,128,1024]{2,1,0:T(8,128)(2,1)} %all-gather.3.cloned.1.call-done), kind=kOutput, calls=%fused_computation.16 | convolution fusion | flops 4297064448 | bytes 10485760 | tf_op jit(solution)/shard_map/rle,ced->crld/dot_general | solution.py:53
  75.3 0.6 copy.83
  75.9 0.1 slice_bitcast_fusion
  76.0 3.6 %collective-permute-start = (bf16[2,256,1024]{2,1,0:T(8,128)(2,1)S(1)}, bf16[2,256,1024]{2,1,0:T(8,128)(2,1)S(1)}, u32[]{:S(2)}, u32[]{:S(2)}) collective-permute-start(bf16[2,256,1024]{2,1,0:T(8,128)(2,1)S(1)} %slice_bitcast_fusion), channel_id=1, source_target_pairs={{0,1},{1,2},{2,3},{3,4},{4,5},{5,6},{6,7},{8,9},{9,10},{10,11},{11... | collective-permute-start | bytes 3145736 | tf_op jit(solution)/shard_map/ppermute | solution.py:15
  79.6 0.1 pad.9.clone
  79.7 0.6 maximum_bitcast_fusion.1
  80.3 1.0 copy.115
  81.3 0.1 copy.113
  81.4 20.8 %collective-permute-done = bf16[2,256,1024]{2,1,0:T(8,128)(2,1)S(1)} collective-permute-done((bf16[2,256,1024]{2,1,0:T(8,128)(2,1)S(1)}, bf16[2,256,1024]{2,1,0:T(8,128)(2,1)S(1)}, u32[]{:S(2)}, u32[]{:S(2)}) %collective-permute-start) | collective-permute-done | bytes 1048608 | tf_op jit(solution)/shard_map/ppermute | solution.py:15
  102.2 2.6 pad_maximum_fusion
  104.8 3.0 copy.86
  107.8 5.0 %copy.85 = bf16[1,5,256,1024]{2,3,1,0:T(8,128)(2,1)} copy(bf16[1,5,256,1024]{3,2,1,0:T(8,128)(2,1)} %get-tuple-element.18) | data formatting | bytes 5242880 | tf_op jit(solution)/shard_map/slice | solution.py:61
  112.7 0.5 fusion.32
  113.2 7.0 %fusion.49 = (f32[5,8,64]{2,1,0:T(8,128)S(1)}, f32[5,8,64,256]{3,2,1,0:T(8,128)S(1)}) fusion(f32[5,8,64,256]{3,2,1,0:T(8,128)S(1)} %fusion.32), kind=kOutput, calls=%fused_computation.77 | output fusion | flops 2621695 | bytes 5253120 | tf_op jit(solution)/shard_map/sub | solution.py:81
  120.2 10.1 %fusion.25 = f32[5,8,128,256]{3,2,1,0:T(8,128)} fusion(bf16[5,64,8,128]{3,2,1,0:T(8,128)(2,1)} %bitcast.121, f32[5,8,64]{2,1,0:T(8,128)S(1)} %get-tuple-element.23, f32[5,8,64,256]{3,2,1,0:T(8,128)} %copy-done.6), kind=kOutput, calls=%fused_computation.46 | convolution fusion | flops 171051776 | bytes 8529920 | tf_op jit(solution)/shard_map/ghqk,gqhd->gkhd/dot_general | solution.py:97
  130.3 6.0 %copy.102 = f32[1,5,256,1024]{3,2,0,1:T(8,128)} copy(f32[1,5,256,1024]{2,3,1,0:T(8,128)} %bitcast.108) | data formatting | bytes 10485760 | tf_op jit(solution)/shard_map/stack | solution.py:101
  136.3 3.0 multiply_reduce_fusion
  139.3 0.9 multiply_convert_fusion
  140.3 3.3 %broadcast_multiply_fusion = f32[5,8,128,256]{3,2,1,0:T(8,128)} fusion(bf16[5,8,64,256]{3,2,1,0:T(8,128)(2,1)S(1)} %multiply_convert_fusion, bf16[5,64,8,128]{3,2,1,0:T(8,128)(2,1)S(1)} %bitcast.107), kind=kOutput, calls=%fused_computation.19 | convolution fusion | flops 169082880 | bytes 7208960 | tf_op jit(solution)/shard_map/ghqk,gqhd->gkhd/dot_general | solution.py:95
  143.5 6.1 %copy.101 = f32[1,5,256,1024]{3,2,0,1:T(8,128)} copy(f32[1,5,256,1024]{2,3,1,0:T(8,128)} %bitcast.104) | data formatting | bytes 10485760 | tf_op jit(solution)/shard_map/stack | solution.py:101
  149.6 1.8 fusion.19
  151.5 1.8 collective-permute-start.1
  153.3 0.8 copy-done.2
  154.0 0.7 fusion.1
  154.8 0.4 copy.104
  155.2 46.3 %collective-permute-done.1 = f32[2,256,1024]{2,1,0:T(8,128)S(1)} collective-permute-done((f32[2,256,1024]{2,1,0:T(8,128)S(1)}, f32[2,256,1024]{2,1,0:T(8,128)S(1)}, u32[]{:S(2)}, u32[]{:S(2)}) %collective-permute-start.1) | collective-permute-done | bytes 2097184 | tf_op jit(solution)/shard_map/ppermute | solution.py:15
  201.5 0.3 fusion.18
  201.8 6.1 %fusion.12 = f32[8,128,1024]{2,1,0:T(8,128)} fusion(bf16[8,128,2,1024]{3,1,0,2:T(8,128)(2,1)S(1)} %bitcast.109, bf16[2,1024,1024]{2,1,0:T(8,128)(2,1)S(1)} %copy-done.10), kind=kOutput, calls=%fused_computation.25 | convolution fusion | flops 4294967296 | bytes 12582912 | tf_op jit(solution)/shard_map/cnd,ced->ne/dot_general | solution.py:106
  207.9 1.7 copy-done.4
  209.6 2.3 fusion.23
  212.0 0.4 copy.94
  212.4 0.1 copy.129
  212.5 0.1 slice.74
  212.7 1.2 copy.95
  213.9 3.5 %all-to-all-start.1 = ((bf16[4,64,1024]{2,0,1:T(4,128)(2,1)}), bf16[4,64,1024]{2,0,1:T(4,128)(2,1)S(1)}, u32[]{:S(2)}, u32[]{:S(2)}) async-start(bf16[4,64,1024]{2,0,1:T(4,128)(2,1)} %copy.95), calls=%async_computation.1 | async-start | bytes 1048576 | tf_op jit(solution)/shard_map/all_to_all | solution.py:100
  217.4 35.4 %reduce-scatter.2.cloned.1.call-done = f32[8,128,256]{2,1,0:T(8,128)} async-done(((f32[8,128,1024]{2,1,0:T(8,128)}), f32[8,128,256]{2,1,0:T(8,128)}) %reduce-scatter.2.cloned.1.call-update) | async-done | bytes 1048592 | tf_op jit(solution)/shard_map/reduce_scatter | solution.py:108
  252.8 1.6 broadcast_in_dim.24
  254.3 2.9 scatter_fusion
  257.2 5.5 %all-to-all-start.2 = ((f32[8,2,128,256]{3,2,1,0:T(8,128)}), f32[8,2,128,256]{3,2,1,0:T(8,128)S(1)}, u32[]{:S(2)}, u32[]{:S(2)}) async-start(f32[8,2,128,256]{3,2,1,0:T(8,128)} %bitcast.32), calls=%async_computation.3 | async-start | bytes 4194304 | tf_op jit(solution)/shard_map/all_to_all | solution.py:112
  262.7 7.9 %fusion.24 = bf16[5,64,8,128]{3,1,2,0:T(8,128)(2,1)S(1)} fusion(bf16[5,256,8,128]{1,3,2,0:T(8,128)(2,1)} %bitcast.112, f32[5,8,64]{2,1,0:T(8,128)S(1)} %get-tuple-element.23, f32[5,8,64,256]{3,2,1,0:T(8,128)} %copy-done.6), kind=kOutput, calls=%fused_computation.39 | convolution fusion | flops 171379456 | bytes 5908480 | tf_op jit(solution)/shard_map/ghqk,gkhd->gqhd/dot_general | solution.py:84
  270.6 0.4 copy.90
  271.1 0.1 copy.130
  271.2 0.9 slice.73
  272.1 0.2 copy.96
  272.3 0.8 copy.112
  273.1 37.9 %all-to-all-done.2 = f32[8,2,128,256]{3,2,1,0:T(8,128)S(1)} async-done(((f32[8,2,128,256]{3,2,1,0:T(8,128)}), f32[8,2,128,256]{3,2,1,0:T(8,128)S(1)}, u32[]{:S(2)}, u32[]{:S(2)}) %all-to-all-start.2) | async-done | bytes 2097184 | tf_op jit(solution)/shard_map/all_to_all | solution.py:112
  311.0 2.2 scatter_fusion.1
  313.2 0.7 slice.106
  (40 shorter events, 0.3 us)
Async XLA Ops:
  7.2 2.6 copy-start
  11.5 33.0 %all-to-all-start = ((bf16[8,2,128,256]{3,2,1,0:T(8,128)(2,1)}), bf16[8,2,128,256]{3,2,1,0:T(8,128)(2,1)S(1)}, u32[]{:S(2)}, u32[]{:S(2)}) async-start(bf16[8,2,128,256]{3,2,1,0:T(8,128)(2,1)} %broadcast_select_fusion), calls=%async_computation | async-start | bytes 2097152 | tf_op jit(solution)/shard_map/all_to_all | solution.py:50
  18.8 49.2 %all-gather.3.cloned.1.call-start = ((), (), s32[]{:S(2)}) async-start(), calls=%async_computation.5 | async-start | bytes 2621440 | tf_op jit(solution)/shard_map/all_gather | solution.py:52
  45.9 206.8 %reduce-scatter.2.cloned.1.call-start = ((), (), s32[]{:S(2)}) async-start(), calls=%async_computation.4 | async-start | bytes 5242880 | tf_op jit(solution)/shard_map/reduce_scatter | solution.py:108
  75.3 4.4 %copy-start.8 = (bf16[256,1024]{1,0:T(8,128)(2,1)S(1)}, bf16[256,1024]{1,0:T(8,128)(2,1)}, u32[]{:S(2)}) copy-start(bf16[256,1024]{1,0:T(8,128)(2,1)} %param.11) | copy-start | bytes 1572868
  75.3 4.4 %copy-start.9 = (bf16[256,1024]{1,0:T(8,128)(2,1)S(1)}, bf16[256,1024]{1,0:T(8,128)(2,1)}, u32[]{:S(2)}) copy-start(bf16[256,1024]{1,0:T(8,128)(2,1)} %param.8) | copy-start | bytes 1572868
  76.0 26.2 %collective-permute-start = (bf16[2,256,1024]{2,1,0:T(8,128)(2,1)S(1)}, bf16[2,256,1024]{2,1,0:T(8,128)(2,1)S(1)}, u32[]{:S(2)}, u32[]{:S(2)}) collective-permute-start(bf16[2,256,1024]{2,1,0:T(8,128)(2,1)S(1)} %slice_bitcast_fusion), channel_id=1, source_target_pairs={{0,1},{1,2},{2,3},{3,4},{4,5},{5,6},{6,7},{8,9},{9,10},{10,11},{11... | collective-permute-start | bytes 3145736 | tf_op jit(solution)/shard_map/ppermute | solution.py:15
  107.8 5.0 %copy-start.3 = (bf16[1,5,256,1024]{2,3,1,0:T(8,128)(2,1)}, bf16[1,5,256,1024]{2,3,1,0:T(8,128)(2,1)S(1)}, u32[]{:S(2)}) copy-start(bf16[1,5,256,1024]{2,3,1,0:T(8,128)(2,1)S(1)} %copy.86) | copy-start | bytes 7864324
  113.2 7.0 %copy-start.6 = (f32[5,8,64,256]{3,2,1,0:T(8,128)}, f32[5,8,64,256]{3,2,1,0:T(8,128)S(1)}, u32[]{:S(2)}) copy-start(f32[5,8,64,256]{3,2,1,0:T(8,128)S(1)} %fusion.32) | copy-start | bytes 7864324
  140.3 3.3 %copy-start.5 = (bf16[5,8,64,256]{3,2,1,0:T(8,128)(2,1)}, bf16[5,8,64,256]{3,2,1,0:T(8,128)(2,1)S(1)}, u32[]{:S(2)}) copy-start(bf16[5,8,64,256]{3,2,1,0:T(8,128)(2,1)S(1)} %multiply_convert_fusion) | copy-start | bytes 3932164
  143.5 9.7 %slice-start = ((s8[5242880]{0:T(1024)(128)(4,1)}), s8[1048576]{0:T(1024)(128)(4,1)S(1)}, s32[]{:S(2)}) async-start(s8[5242880]{0:T(1024)(128)(4,1)} %bitcast.98), calls=%async_computation.6 | async-start | bytes 2097152
  149.6 3.6 %slice-start.1 = ((s8[5242880]{0:T(1024)(128)(4,1)}), s8[4194304]{0:T(1024)(128)(4,1)S(1)}, s32[]{:S(2)}) async-start(s8[5242880]{0:T(1024)(128)(4,1)} %bitcast.98), calls=%async_computation.7 | async-start | bytes 8388608
  149.6 4.4 %copy-start.2 = (f32[1,5,256,1024]{3,2,0,1:T(8,128)S(1)}, f32[1,5,256,1024]{3,2,0,1:T(8,128)}, u32[]{:S(2)}) copy-start(f32[1,5,256,1024]{3,2,0,1:T(8,128)} %copy.101) | copy-start | bytes 15728644
  151.5 50.0 %collective-permute-start.1 = (f32[2,256,1024]{2,1,0:T(8,128)S(1)}, f32[2,256,1024]{2,1,0:T(8,128)S(1)}, u32[]{:S(2)}, u32[]{:S(2)}) collective-permute-start(f32[2,256,1024]{2,1,0:T(8,128)S(1)} %fusion.19), channel_id=1, source_target_pairs={{1,0},{2,1},{3,2},{4,3},{5,4},{6,5},{7,6},{9,8},{10,9},{11,10},{12... | collective-permute-start | bytes 6291464 | tf_op jit(solution)/shard_map/ppermute | solution.py:15
  155.2 46.6 %copy-start.10 = (bf16[2,1024,1024]{2,1,0:T(8,128)(2,1)S(1)}, bf16[2,1024,1024]{2,1,0:T(8,128)(2,1)}, u32[]{:S(2)}) copy-start(bf16[2,1024,1024]{2,1,0:T(8,128)(2,1)} %param.10) | copy-start | bytes 12582916
  207.9 1.7 copy-start.4
  213.9 43.3 %all-to-all-start.1 = ((bf16[4,64,1024]{2,0,1:T(4,128)(2,1)}), bf16[4,64,1024]{2,0,1:T(4,128)(2,1)S(1)}, u32[]{:S(2)}, u32[]{:S(2)}) async-start(bf16[4,64,1024]{2,0,1:T(4,128)(2,1)} %copy.95), calls=%async_computation.1 | async-start | bytes 1048576 | tf_op jit(solution)/shard_map/all_to_all | solution.py:100
  252.8 1.6 copy-start.7
  257.2 53.8 %all-to-all-start.2 = ((f32[8,2,128,256]{3,2,1,0:T(8,128)}), f32[8,2,128,256]{3,2,1,0:T(8,128)S(1)}, u32[]{:S(2)}, u32[]{:S(2)}) async-start(f32[8,2,128,256]{3,2,1,0:T(8,128)} %bitcast.32), calls=%async_computation.3 | async-start | bytes 4194304 | tf_op jit(solution)/shard_map/all_to_all | solution.py:112
  311.0 2.9 copy-start.1
Sparse Core Ops, SparseCore 0:
  46.1 21.8 all-gather.2
  208.0 44.6 reduce-scatter.1
where the time goes:
time: 322 us; the launch traced here: 321 us
  waiting for transfers between devices  188 us (58%)
  matrix products  40.4 us (13%)
  local copies, waits for them, and re-layouts  38.5 us (12%)
  starting transfers between devices  21.8 us (7%)
  other arithmetic  17.8 us (6%)
  between operations  14.4 us (4%)
    ppermute x2, waiting for transfers between devices, passed_along(): return lax.ppermute(array, axis, pairs)  67 us
    all_to_all x1, waiting for transfers between devices, per_device(): lax.all_to_all(outgoing_grad, 'seq', split_axis=0, concat_axis=0, tiled=T...  37.9 us
    reduce_scatter x1, waiting for transfers between devices, per_device(): lax.psum_scatter(term, 'head', scatter_dimension=2, tiled=True)  35.4 us
    all_to_all x1, waiting for transfers between devices, per_device(): lax.all_to_all(outgoing, 'seq', split_axis=0, concat_axis=0, tiled=True)  25.7 us
    all_gather x1, waiting for transfers between devices, per_device(): features = lax.all_gather(picked, 'head', axis=2, tiled=True)  22 us
    another operation x2, local copies, waits for them, and re-layouts, per_device(): jnp.stack([kgrad, vgrad], 0).reshape(2, groups, window, local_width)  12.1 us
    dot_general x1, matrix products, per_device(): jnp.einsum('ghqk,gqhd->gkhd', probs_half, grad_pad, preferred_element_typ...  10.1 us
    dot_general x1, matrix products, per_device(): jnp.einsum('ghqk,gkhd->gqhd', probs_half, value_block, preferred_element_...  7.86 us
  transfers between devices with their start and end apart: 7, of which 6 were waited for; matrix products, arithmetic and copies ran while one was open for 7% of the time, Pallas kernels for 0%

commit v1 on v0

--- a/solution.py
+++ b/solution.py
@@ -7,6 +7,22 @@
 SPAN = 64
 NEIGHBOURS = 2
 NEIGHBOUR_LEN = 128
+
+
+def summed_both_ways(value, axis, dim, contribution):
+    length, index, extent = (lax.axis_size(axis), lax.axis_index(axis), value.shape[dim])
+    right = [(i, (i + 1) % length) for i in range(length)]
+    left = [(i, (i - 1) % length) for i in range(length)]
+    middle = length // 2
+    from_left = from_right = value
+    total = contribution(value, index * extent)
+    for lap in range(1, middle + 1):
+        from_left = lax.ppermute(from_left, axis, right)
+        if lap < length - middle:
+            from_right = lax.ppermute(from_right, axis, left)
+            total = total + contribution(from_right, (index + lap) % length * extent)
+        total = total + contribution(from_left, (index - lap) % length * extent)
+    return total
 
 
 def passed_along(array, axis, by):
@@ -49,9 +65,16 @@
     outgoing = outgoing.reshape(seq_count, capacity, NEIGHBOUR_LEN, slice_width)
     incoming = lax.all_to_all(outgoing, "seq", split_axis=0, concat_axis=0, tiled=True)
     picked = incoming.reshape(seq_count * capacity, NEIGHBOUR_LEN, slice_width)[slot_place]
-    features = lax.all_gather(picked, "head", axis=2, tiled=True)
-    projected = jnp.einsum(
-        "rle,ced->crld", features, kv_weight, preferred_element_type=jnp.float32
+    projected = summed_both_ways(
+        picked,
+        "head",
+        2,
+        lambda shard, start: jnp.einsum(
+            "rle,ced->crld",
+            shard,
+            lax.dynamic_slice_in_dim(kv_weight, start, shard.shape[2], axis=1),
+            preferred_element_type=jnp.float32,
+        ),
     ).astype(jnp.bfloat16)
     by_span = projected.reshape(2, spans_local, window, local_width)
     carried = passed_along(by_span[:, -1], "seq", 1)

time: 322 us -> 311 us (0.966)
  waiting for transfers between devices: 188 us -> 166 us
  matrix products: 40.4 us -> 51.8 us
    all_gather x1 -> x0, waiting for transfers between devices: 22 us -> none  [per_device(): features = lax.all_gather(picked, 'head', axis=2, tiled=True)]
    dot_general x1 -> x4, matrix products: 7.31 us -> 19.5 us  [per_device(): jnp.einsum('rle,ced->crld', shard, lax.dynamic_slice_in_dim(kv_weight, st...]
    ppermute x0 -> x3, waiting for transfers between devices: none -> 8.14 us  [the longest x2 8.14 us: summed_both_ways(): from_left = lax.ppermute(from_left, axis, right)]
    slice x2 -> x1, local copies, waits for them, and re-layouts: 7.93 us -> 0.07 us  [per_device(): carried = passed_along(by_span[:, -1], 'seq', 1)]
    ppermute x2, waiting for transfers between devices: 67 us -> 59.7 us  [passed_along(): return lax.ppermute(array, axis, pairs)]
    reshape x0 -> x1, local copies, waits for them, and re-layouts: none -> 6.21 us  [per_device(): by_span = projected.reshape(2, spans_local, window, local_width)]
    sub x1, other arithmetic: 6.98 us -> 2.31 us  [per_device(): expo = jnp.exp(scores - top)]
    unnamed x32 -> x37, local copies, waits for them, and re-layouts: 5.43 us -> 9.72 us
  transfers between devices with their start and end apart: 7 -> 9, of which waited for: 6 -> 6; matrix products, arithmetic and copies ran while one was open for 7% -> 13% of each run, Pallas kernels for 0% -> 0%
where the time goes in v1:
time: 311 us; the launch traced here: 310 us
  waiting for transfers between devices  166 us (53%)
  matrix products  51.8 us (17%)
  local copies, waits for them, and re-layouts  39.6 us (13%)
  starting transfers between devices  23.6 us (8%)
  other arithmetic  15 us (5%)
  between operations  14.5 us (5%)
    ppermute x2, waiting for transfers between devices, passed_along(): return lax.ppermute(array, axis, pairs)  59.7 us
    all_to_all x1, waiting for transfers between devices, per_device(): lax.all_to_all(outgoing_grad, 'seq', split_axis=0, concat_axis=0, tiled=T...  37.9 us
    reduce_scatter x1, waiting for transfers between devices, per_device(): lax.psum_scatter(term, 'head', scatter_dimension=2, tiled=True)  34.1 us
    all_to_all x1, waiting for transfers between devices, per_device(): lax.all_to_all(outgoing, 'seq', split_axis=0, concat_axis=0, tiled=True)  25.7 us
    dot_general x4, matrix products, per_device(): jnp.einsum('rle,ced->crld', shard, lax.dynamic_slice_in_dim(kv_weight, st...  19.5 us
    another operation x2, local copies, waits for them, and re-layouts, per_device(): jnp.stack([kgrad, vgrad], 0).reshape(2, groups, window, local_width)  12.1 us
    unnamed x37, local copies, waits for them, and re-layouts  9.72 us
    dot_general x1, matrix products, per_device(): jnp.einsum('ghqk,gqhd->gkhd', probs_half, grad_pad, preferred_element_typ...  8.37 us
  transfers between devices with their start and end apart: 9, of which 6 were waited for; matrix products, arithmetic and copies ran while one was open for 13% of the time, Pallas kernels for 0%

profile of v1, /device:TPU:0, one launch (start us, length us, event | category | flops | bytes accessed | tf_op | source)
XLA Modules:
  0.0 309.9 jit_solution(15956934705859048028)
XLA Ops:
  7.2 0.8 copy.73
  8.1 0.3 convert_reduce_fusion
  8.4 0.8 copy.75
  9.2 0.2 convert_reduce_fusion.1
  9.4 0.1 copy.74
  9.5 0.1 gt.40
  9.8 0.6 gather_fusion
  10.4 1.1 broadcast_select_fusion
  11.5 7.3 %all-to-all-start = ((bf16[8,2,128,256]{3,2,1,0:T(8,128)(2,1)}), bf16[8,2,128,256]{3,2,1,0:T(8,128)(2,1)S(1)}, u32[]{:S(2)}, u32[]{:S(2)}) async-start(bf16[8,2,128,256]{3,2,1,0:T(8,128)(2,1)} %broadcast_select_fusion), calls=%async_computation | async-start | bytes 2097152 | tf_op jit(solution)/shard_map/all_to_all | solution.py:66
  18.9 25.7 %all-to-all-done = bf16[8,2,128,256]{3,2,1,0:T(8,128)(2,1)S(1)} async-done(((bf16[8,2,128,256]{3,2,1,0:T(8,128)(2,1)}), bf16[8,2,128,256]{3,2,1,0:T(8,128)(2,1)S(1)}, u32[]{:S(2)}, u32[]{:S(2)}) %all-to-all-start) | async-done | bytes 1048608 | tf_op jit(solution)/shard_map/all_to_all | solution.py:66
  44.6 0.6 gather_fusion.1
  45.3 1.7 collective-permute-start
  46.9 2.5 fusion.25
  49.4 8.1 %collective-permute-done.1 = bf16[8,128,256]{2,1,0:T(8,128)(2,1)S(1)} collective-permute-done((bf16[8,128,256]{2,1,0:T(8,128)(2,1)S(1)}, bf16[8,128,256]{2,1,0:T(8,128)(2,1)S(1)}, u32[]{:S(2)}, u32[]{:S(2)}) %collective-permute-start.1) | collective-permute-done | bytes 524320 | tf_op jit(solution)/shard_map/ppermute | solution.py:20
  57.6 0.2 collective-permute-start.2
  57.7 4.5 %fusion.21 = f32[2,1024,8,128]{1,3,2,0:T(8,128)} fusion(bf16[2,1024,1024]{2,1,0:T(8,128)(2,1)S(1)} %copy-done.9, s32[]{:T(128)S(6)} %select_n.87, bf16[8,128,256]{2,1,0:T(8,128)(2,1)S(1)} %collective-permute-done.1), kind=kOutput, calls=%fused_computation.38 | convolution fusion | flops 1073741824 | bytes 9961476 | tf_op jit(solution)/shard_map/rle,ced->crld/dot_general | solution.py:72
  62.2 4.5 %fusion.23 = f32[2,1024,8,128]{1,3,2,0:T(8,128)} fusion(bf16[2,1024,1024]{2,1,0:T(8,128)(2,1)S(1)} %copy-done.9, s32[]{:T(128)S(6)} %select_n.85, bf16[8,128,256]{2,1,0:T(8,128)(2,1)S(1)} %collective-permute-done), kind=kOutput, calls=%fused_computation.40 | convolution fusion | flops 1073741824 | bytes 9961476 | tf_op jit(solution)/shard_map/rle,ced->crld/dot_general | solution.py:72
  66.7 8.0 %add_convert_fusion = bf16[2,1024,8,128]{1,3,2,0:T(8,128)(2,1)S(1)} fusion(f32[2,1024,8,128]{1,3,2,0:T(8,128)} %fusion.21, f32[2,1024,8,128]{1,3,2,0:T(8,128)S(1)} %fusion.25, f32[2,1024,8,128]{1,3,2,0:T(8,128)} %fusion.23, bf16[2,1024,1024]{2,1,0:T(8,128)(2,1)} %param.10, s32[]{:T(128)S(6)} %select_n.89, bf16[8,128,256]{2,1,0:T(8,128)(2,1)S(1)} %collective-permute-done.2), kind=kOutput, calls=%fused_computation.10 | convolution fusion | flops 1082130432 | bytes 30932996 | tf_op jit(solution)/shard_map/rle,ced->crld/dot_general | solution.py:72
  74.8 1.9 copy-done.5
  76.8 1.3 copy.106
  78.1 3.6 %collective-permute-start.3 = (bf16[2,256,1024]{1,2,0:T(8,128)(2,1)}, bf16[2,256,1024]{1,2,0:T(8,128)(2,1)S(1)}, u32[]{:S(2)}, u32[]{:S(2)}) collective-permute-start(bf16[2,256,1024]{1,2,0:T(8,128)(2,1)} %bitcast.140), channel_id=1, source_target_pairs={{0,1},{1,2},{2,3},{3,4},{4,5},{5,6},{6,7},{8,9},{9,10},{10,11},{11... | collective-permute-start | bytes 3145736 | tf_op jit(solution)/shard_map/ppermute | solution.py:31
  81.8 1.7 maximum_bitcast_fusion.1
  83.4 0.1 copy.108
  83.6 1.0 copy.110
  84.5 6.2 %copy.78 = bf16[2,4,256,1024]{2,3,1,0:T(8,128)(2,1)} copy(bf16[2,4,256,1024]{3,2,1,0:T(8,128)(2,1)} %bitcast.122) | data formatting | bytes 8388608 | tf_op jit(solution)/shard_map/reshape | solution.py:79
  90.8 13.0 %collective-permute-done.3 = bf16[2,256,1024]{1,2,0:T(8,128)(2,1)S(1)} collective-permute-done((bf16[2,256,1024]{1,2,0:T(8,128)(2,1)}, bf16[2,256,1024]{1,2,0:T(8,128)(2,1)S(1)}, u32[]{:S(2)}, u32[]{:S(2)}) %collective-permute-start.3) | collective-permute-done | bytes 1048608 | tf_op jit(solution)/shard_map/ppermute | solution.py:31
  103.7 3.5 %pad_maximum_fusion = (bf16[1,5,256,1024]{2,3,1,0:T(8,128)(2,1)S(1)}, bf16[1,5,256,1024]{2,3,1,0:T(8,128)(2,1)}) fusion(bf16[2,4,256,1024]{2,3,1,0:T(8,128)(2,1)} %copy.78, bf16[2,1,256,1024]{2,3,1,0:T(8,128)(2,1)S(1)} %bitcast.139), kind=kLoop, calls=%fused_computation.16 | loop fusion | flops 2621440 | bytes 10485760 | tf_op jit(solution)/shard_map/concatenate | solution.py:81
  107.2 0.5 fusion.38
  107.7 1.0 copy-done.3
  108.7 2.3 fusion.63
  111.0 8.4 %fusion.31 = f32[5,8,128,256]{3,2,1,0:T(8,128)} fusion(bf16[5,64,8,128]{3,2,1,0:T(8,128)(2,1)} %bitcast.141, f32[5,8,64]{2,1,0:T(8,128)S(1)} %get-tuple-element.23, f32[5,8,64,256]{3,2,1,0:T(8,128)S(1)} %fusion.38), kind=kOutput, calls=%fused_computation.53 | convolution fusion | flops 171051776 | bytes 8529920 | tf_op jit(solution)/shard_map/ghqk,gqhd->gkhd/dot_general | solution.py:120
  119.4 3.9 %multiply_reduce_fusion = (f32[5,8,64]{2,1,0:T(8,128)S(1)}, f32[5,8,64,256]{3,2,1,0:T(8,128)S(1)}) fusion(f32[5,8,64,256]{3,2,1,0:T(8,128)} %get-tuple-element.24, f32[5,8,64]{2,1,0:T(8,128)S(1)} %get-tuple-element.23, bf16[5,256,8,128]{1,3,2,0:T(8,128)(2,1)} %bitcast.130, bf16[5,64,8,128]{3,2,1,0:T(8,128)(2,1)} %bitcast.142), kind=kOutput, calls=%fused_computation.19 | convolution fusion | flops 169735680 | bytes 8540160 | tf_op jit(solution)/shard_map/gqhd,gkhd->ghqk/dot_general | solution.py:111
  123.3 0.9 multiply_convert_fusion
  124.2 3.3 %broadcast_multiply_fusion = f32[5,8,128,256]{3,2,1,0:T(8,128)} fusion(bf16[5,8,64,256]{3,2,1,0:T(8,128)(2,1)S(1)} %multiply_convert_fusion, bf16[5,64,8,128]{3,2,1,0:T(8,128)(2,1)S(1)} %bitcast.126), kind=kOutput, calls=%fused_computation.17 | convolution fusion | flops 169082880 | bytes 7208960 | tf_op jit(solution)/shard_map/ghqk,gqhd->gkhd/dot_general | solution.py:118
  127.5 6.0 %copy.93 = f32[1,5,256,1024]{3,2,0,1:T(8,128)} copy(f32[1,5,256,1024]{2,3,1,0:T(8,128)} %bitcast.123) | data formatting | bytes 10485760 | tf_op jit(solution)/shard_map/stack | solution.py:124
  133.5 6.1 %copy.94 = f32[1,5,256,1024]{3,2,0,1:T(8,128)} copy(f32[1,5,256,1024]{2,3,1,0:T(8,128)} %bitcast.127) | data formatting | bytes 10485760 | tf_op jit(solution)/shard_map/stack | solution.py:124
  139.6 1.8 fusion.15
  141.4 1.8 collective-permute-start.4
  143.2 0.8 copy-done.2
  144.0 0.7 fusion.1
  144.7 0.4 copy.96
  145.2 46.7 %collective-permute-done.4 = f32[2,256,1024]{2,1,0:T(8,128)S(1)} collective-permute-done((f32[2,256,1024]{2,1,0:T(8,128)S(1)}, f32[2,256,1024]{2,1,0:T(8,128)S(1)}, u32[]{:S(2)}, u32[]{:S(2)}) %collective-permute-start.4) | collective-permute-done | bytes 2097184 | tf_op jit(solution)/shard_map/ppermute | solution.py:31
  191.9 0.3 fusion.14
  192.2 6.1 %fusion.8 = f32[8,128,1024]{2,1,0:T(8,128)} fusion(bf16[8,128,2,1024]{3,1,0,2:T(8,128)(2,1)S(1)} %bitcast.128, bf16[2,1024,1024]{2,1,0:T(8,128)(2,1)S(1)} %copy-done.10), kind=kOutput, calls=%fused_computation.23 | convolution fusion | flops 4294967296 | bytes 12582912 | tf_op jit(solution)/shard_map/cnd,ced->ne/dot_general | solution.py:129
  198.4 1.7 copy-done.4
  200.1 2.3 fusion.18
  202.4 0.4 copy.86
  202.9 0.1 copy.124
  203.0 0.1 slice.74
  203.1 1.2 copy.87
  204.3 3.5 %all-to-all-start.1 = ((bf16[4,64,1024]{2,0,1:T(4,128)(2,1)}), bf16[4,64,1024]{2,0,1:T(4,128)(2,1)S(1)}, u32[]{:S(2)}, u32[]{:S(2)}) async-start(bf16[4,64,1024]{2,0,1:T(4,128)(2,1)} %copy.87), calls=%async_computation.1 | async-start | bytes 1048576 | tf_op jit(solution)/shard_map/all_to_all | solution.py:123
  207.9 34.1 %reduce-scatter.2.cloned.1.call-done = f32[8,128,256]{2,1,0:T(8,128)} async-done(((f32[8,128,1024]{2,1,0:T(8,128)}), f32[8,128,256]{2,1,0:T(8,128)}) %reduce-scatter.2.cloned.1.call-update) | async-done | bytes 1048592 | tf_op jit(solution)/shard_map/reduce_scatter | solution.py:131
  242.0 1.6 broadcast_in_dim.24
  243.5 2.9 scatter_fusion
  246.4 5.5 %all-to-all-start.2 = ((f32[8,2,128,256]{3,2,1,0:T(8,128)}), f32[8,2,128,256]{3,2,1,0:T(8,128)S(1)}, u32[]{:S(2)}, u32[]{:S(2)}) async-start(f32[8,2,128,256]{3,2,1,0:T(8,128)} %bitcast.43), calls=%async_computation.3 | async-start | bytes 4194304 | tf_op jit(solution)/shard_map/all_to_all | solution.py:135
  251.9 7.9 %fusion.19 = bf16[5,64,8,128]{3,1,2,0:T(8,128)(2,1)S(1)} fusion(bf16[5,256,8,128]{1,3,2,0:T(8,128)(2,1)} %bitcast.131, f32[5,8,64]{2,1,0:T(8,128)S(1)} %get-tuple-element.23, f32[5,8,64,256]{3,2,1,0:T(8,128)} %copy-done.7), kind=kOutput, calls=%fused_computation.36 | convolution fusion | flops 171379456 | bytes 5908480 | tf_op jit(solution)/shard_map/ghqk,gkhd->gqhd/dot_general | solution.py:107
  259.8 0.5 copy.82
  260.2 0.1 copy.125
  260.4 0.9 slice.73
  261.3 0.2 copy.88
  261.4 0.8 copy.107
  262.3 37.9 %all-to-all-done.2 = f32[8,2,128,256]{3,2,1,0:T(8,128)S(1)} async-done(((f32[8,2,128,256]{3,2,1,0:T(8,128)}), f32[8,2,128,256]{3,2,1,0:T(8,128)S(1)}, u32[]{:S(2)}, u32[]{:S(2)}) %all-to-all-start.2) | async-done | bytes 2097184 | tf_op jit(solution)/shard_map/all_to_all | solution.py:135
  300.2 2.2 scatter_fusion.1
  302.4 0.7 slice.105
  (49 shorter events, 0.7 us)
Async XLA Ops:
  7.2 2.6 copy-start
  11.5 33.0 %all-to-all-start = ((bf16[8,2,128,256]{3,2,1,0:T(8,128)(2,1)}), bf16[8,2,128,256]{3,2,1,0:T(8,128)(2,1)S(1)}, u32[]{:S(2)}, u32[]{:S(2)}) async-start(bf16[8,2,128,256]{3,2,1,0:T(8,128)(2,1)} %broadcast_select_fusion), calls=%async_computation | async-start | bytes 2097152 | tf_op jit(solution)/shard_map/all_to_all | solution.py:66
  18.8 223.2 %reduce-scatter.2.cloned.1.call-start = ((), (), s32[]{:S(2)}) async-start(), calls=%async_computation.4 | async-start | bytes 5242880 | tf_op jit(solution)/shard_map/reduce_scatter | solution.py:131
  45.1 12.4 %collective-permute-start.1 = (bf16[8,128,256]{2,1,0:T(8,128)(2,1)S(1)}, bf16[8,128,256]{2,1,0:T(8,128)(2,1)S(1)}, u32[]{:S(2)}, u32[]{:S(2)}) collective-permute-start(bf16[8,128,256]{2,1,0:T(8,128)(2,1)S(1)} %gather_fusion.1), channel_id=1, source_target_pairs={{0,8},{8,16},{16,24},{24,0},{1,9},{9,17},{17,25},{25,1},{2,10},{10... | collective-permute-start | bytes 1572872 | tf_op jit(solution)/shard_map/ppermute | solution.py:20
  45.3 12.5 %copy-start.9 = (bf16[2,1024,1024]{2,1,0:T(8,128)(2,1)S(1)}, bf16[2,1024,1024]{2,1,0:T(8,128)(2,1)}, u32[]{:S(2)}) copy-start(bf16[2,1024,1024]{2,1,0:T(8,128)(2,1)} %param.10) | copy-start | bytes 12582916
  45.3 17.0 %collective-permute-start = (bf16[8,128,256]{2,1,0:T(8,128)(2,1)S(1)}, bf16[8,128,256]{2,1,0:T(8,128)(2,1)S(1)}, u32[]{:S(2)}, u32[]{:S(2)}) collective-permute-start(bf16[8,128,256]{2,1,0:T(8,128)(2,1)S(1)} %gather_fusion.1), channel_id=1, source_target_pairs={{0,24},{8,0},{16,8},{24,16},{1,25},{9,1},{17,9},{25,17},{2,26},{10... | collective-permute-start | bytes 1572872 | tf_op jit(solution)/shard_map/ppermute | solution.py:22
  57.6 9.2 %collective-permute-start.2 = (bf16[8,128,256]{2,1,0:T(8,128)(2,1)S(1)}, bf16[8,128,256]{2,1,0:T(8,128)(2,1)S(1)}, u32[]{:S(2)}, u32[]{:S(2)}) collective-permute-start(bf16[8,128,256]{2,1,0:T(8,128)(2,1)S(1)} %collective-permute-done.1), channel_id=1, source_target_pairs={{0,8},{8,16},{16,24},{24,0},{1,9},{9,17},{17,25},{25,1},{2,10},{10... | collective-permute-start | bytes 1572872 | tf_op jit(solution)/shard_map/ppermute | solution.py:20
  74.8 1.9 copy-start.5
  74.8 7.0 %copy-start.12 = (bf16[256,1024]{1,0:T(8,128)(2,1)S(1)}, bf16[256,1024]{1,0:T(8,128)(2,1)}, u32[]{:S(2)}) copy-start(bf16[256,1024]{1,0:T(8,128)(2,1)} %param.11) | copy-start | bytes 1572868
  78.1 25.6 %collective-permute-start.3 = (bf16[2,256,1024]{1,2,0:T(8,128)(2,1)}, bf16[2,256,1024]{1,2,0:T(8,128)(2,1)S(1)}, u32[]{:S(2)}, u32[]{:S(2)}) collective-permute-start(bf16[2,256,1024]{1,2,0:T(8,128)(2,1)} %bitcast.140), channel_id=1, source_target_pairs={{0,1},{1,2},{2,3},{3,4},{4,5},{5,6},{6,7},{8,9},{9,10},{10,11},{11... | collective-permute-start | bytes 3145736 | tf_op jit(solution)/shard_map/ppermute | solution.py:31
  107.2 1.5 copy-start.3
  108.7 2.3 copy-start.7
  119.4 3.9 %copy-start.8 = (f32[5,8,64,256]{3,2,1,0:T(8,128)S(1)}, f32[5,8,64,256]{3,2,1,0:T(8,128)}, u32[]{:S(2)}) copy-start(f32[5,8,64,256]{3,2,1,0:T(8,128)} %get-tuple-element.24) | copy-start | bytes 7864324
  124.2 3.3 %copy-start.6 = (bf16[5,8,64,256]{3,2,1,0:T(8,128)(2,1)}, bf16[5,8,64,256]{3,2,1,0:T(8,128)(2,1)S(1)}, u32[]{:S(2)}) copy-start(bf16[5,8,64,256]{3,2,1,0:T(8,128)(2,1)S(1)} %multiply_convert_fusion) | copy-start | bytes 3932164
  133.5 9.7 %slice-start = ((s8[5242880]{0:T(1024)(128)(4,1)}), s8[1048576]{0:T(1024)(128)(4,1)S(1)}, s32[]{:S(2)}) async-start(s8[5242880]{0:T(1024)(128)(4,1)} %bitcast.117), calls=%async_computation.5 | async-start | bytes 2097152
  139.6 3.6 %slice-start.1 = ((s8[5242880]{0:T(1024)(128)(4,1)}), s8[4194304]{0:T(1024)(128)(4,1)S(1)}, s32[]{:S(2)}) async-start(s8[5242880]{0:T(1024)(128)(4,1)} %bitcast.117), calls=%async_computation.6 | async-start | bytes 8388608
  139.6 4.4 %copy-start.2 = (f32[1,5,256,1024]{3,2,0,1:T(8,128)S(1)}, f32[1,5,256,1024]{3,2,0,1:T(8,128)}, u32[]{:S(2)}) copy-start(f32[1,5,256,1024]{3,2,0,1:T(8,128)} %copy.94) | copy-start | bytes 15728644
  141.4 50.5 %collective-permute-start.4 = (f32[2,256,1024]{2,1,0:T(8,128)S(1)}, f32[2,256,1024]{2,1,0:T(8,128)S(1)}, u32[]{:S(2)}, u32[]{:S(2)}) collective-permute-start(f32[2,256,1024]{2,1,0:T(8,128)S(1)} %fusion.15), channel_id=1, source_target_pairs={{1,0},{2,1},{3,2},{4,3},{5,4},{6,5},{7,6},{9,8},{10,9},{11,10},{12... | collective-permute-start | bytes 6291464 | tf_op jit(solution)/shard_map/ppermute | solution.py:31
  145.2 47.0 %copy-start.10 = (bf16[2,1024,1024]{2,1,0:T(8,128)(2,1)S(1)}, bf16[2,1024,1024]{2,1,0:T(8,128)(2,1)}, u32[]{:S(2)}) copy-start(bf16[2,1024,1024]{2,1,0:T(8,128)(2,1)} %param.10) | copy-start | bytes 12582916
  198.3 1.7 copy-start.4
  204.3 42.1 %all-to-all-start.1 = ((bf16[4,64,1024]{2,0,1:T(4,128)(2,1)}), bf16[4,64,1024]{2,0,1:T(4,128)(2,1)S(1)}, u32[]{:S(2)}, u32[]{:S(2)}) async-start(bf16[4,64,1024]{2,0,1:T(4,128)(2,1)} %copy.87), calls=%async_computation.1 | async-start | bytes 1048576 | tf_op jit(solution)/shard_map/all_to_all | solution.py:123
  242.0 1.6 copy-start.11
  246.4 53.7 %all-to-all-start.2 = ((f32[8,2,128,256]{3,2,1,0:T(8,128)}), f32[8,2,128,256]{3,2,1,0:T(8,128)S(1)}, u32[]{:S(2)}, u32[]{:S(2)}) async-start(f32[8,2,128,256]{3,2,1,0:T(8,128)} %bitcast.43), calls=%async_computation.3 | async-start | bytes 4194304 | tf_op jit(solution)/shard_map/all_to_all | solution.py:135
  300.2 2.9 copy-start.1
Sparse Core Ops, SparseCore 0:
  198.5 43.4 reduce-scatter.1
